TPU v7x, 256 devices: a whole 4x4x8 slice. The times are simulated.
256 devices in a mesh: row: 8 (over y, core), col: 32 (over z, x).
Axes of the slice: x: 4, y: 4, z: 8, core: 2. Of those that a mesh axis runs over, the one named last changes fastest.
Arguments:
- solution: float32 [8, 32, 16, 128, 128], P('row', 'col'), may hold values from -6 to 6
- residual: float32 [8, 32, 16, 128, 128], P('row', 'col'), may hold values from -6 to 6, as said below
- prev_direction: float32 [8, 32, 16, 128, 128], P('row', 'col'), may hold values from -6 to 6, as said below
- prev_dot: float32 [128], replicated, may hold values from 262144 to 1048576
- face_lists: int32 [8, 32, 4, 4], P('row', 'col'), may hold values from 0 to 16, as said below
- multiplicity: int32 [8, 32, 16], P('row', 'col'), may hold values from 1 to 2, as said below
- block_pattern: int32 [8, 32, 16, 3], P('row', 'col'), may hold values from 0 to 15, as said below
- schur: float32 [8, 32, 16, 3, 128, 128], P('row', 'col'), may hold values from -1 to 4, as said below
- neumann_inverse: float32 [8, 32, 16, 3, 128, 128], P('row', 'col'), may hold values from 0 to 2, as said below
- coarse_basis: float32 [8, 32, 8, 2048], P('row', 'col'), may hold values from -0.25 to 0.25
- primal_map: int32 [8, 32, 8], P('row', 'col'), may hold values from 0 to 1023, all different within a row
- coarse_inverse: float32 [1024, 1024], P('col'), may hold values from -1 to 1, as said below
Outputs:
- new_solution: float32 [8, 32, 16, 128, 128], P('row', 'col')
- new_residual: float32 [8, 32, 16, 128, 128], P('row', 'col')
- direction: float32 [8, 32, 16, 128, 128], P('row', 'col')
Inputs may be any that keep to these rules, and one draw needn't show every extreme that they name: face_lists[i, j, f, k] names the interface blocks that subdomain (i, j) shares with its neighbour across face f (0 toward row i-1, 1 toward row i+1, 2 toward column j-1, 3 toward column j+1); slot k of a face names the same unknowns as slot k of the neighbour's list for the facing face, and both lists have the same length, 1 to 4 blocks, none on faces at the grid's edge; unused slots hold 16; no block lies on two faces; some face holds 4 blocks. multiplicity is 2 for blocks named in face_lists and 1 for the others. block_pattern[i, j, b, 0] = b; the two other entries of block row b are two other blocks, each of which lists b in turn. `schur`: each subdomain's Schur complement is symmetric positive definite, with positive diagonal and no positive entry off it. `neumann_inverse`: each subdomain's local solve matrix is symmetric positive definite. `coarse_inverse`: symmetric positive definite. `residual`: copies of an unknown held by two subdomains (slot k of facing lists) are equal. `prev_direction`: copies of an unknown held by two subdomains (slot k of facing lists) are equal.
All inputs are finite; a program needn't handle non-finite values.
Results may differ from a plain program's by a relative error of at most 0.0003.
Values sent between devices are 32-bit elements; how exact they have to be, the bound alone decides.
A program may use at most 128 MiB of HBM per device.

v0:
```python
import jax
import jax.numpy as jnp
from jax import lax
from jax.sharding import PartitionSpec as P

HIGH = lax.Precision.HIGHEST


def extended(cells, sides, width):
    for axis, dim in sides:
        count = lax.axis_size(axis)
        ends = count - 1
        head = lax.slice_in_dim(cells, 0, width, axis=dim)
        tail = lax.slice_in_dim(cells, cells.shape[dim] - width, cells.shape[dim], axis=dim)
        cells = jnp.concatenate(
            [
                lax.ppermute(tail, axis, [(i, (i + 1) % count) for i in range(ends)]),
                cells,
                lax.ppermute(head, axis, [((i + 1) % count, i) for i in range(ends)]),
            ],
            axis=dim,
        )
    return cells


def block_product(blocks, pattern, values_in):
    stacked_count, block_count, dofs, cases = values_in.shape
    gathered = jnp.take(values_in, pattern.reshape(-1), axis=1)
    gathered = gathered.reshape(stacked_count, block_count, pattern.shape[1], dofs, cases)
    return jnp.einsum("bkij,vbkjn->vbin", blocks, gathered, precision=HIGH)


def assemble(values_in, faces):
    stacked_count, block_count, dofs, cases = values_in.shape
    flattened = values_in.reshape(stacked_count, block_count, dofs * cases)
    indicator = (faces[..., None] == jnp.arange(block_count)).astype(jnp.float32)
    face_values = jnp.einsum("fkb,vbc->fvkc", indicator, flattened, precision=HIGH)
    row_faces = extended(face_values[0:2], (("row", 0),), 1)
    col_faces = extended(face_values[2:4], (("col", 0),), 1)
    received = jnp.stack([row_faces[0], row_faces[3], col_faces[0], col_faces[3]])
    added = jnp.einsum("fkb,fvkc->vbc", indicator, received, precision=HIGH)
    return (flattened + added).reshape(values_in.shape)


def precondition(residual, weight, faces, pattern, neumann, basis, primal_map, inverse_rows):
    scaled = residual * weight
    local_term = block_product(neumann, pattern, scaled[None])[0]
    cases = residual.shape[-1]
    coarse_local = jnp.dot(basis, scaled.reshape(-1, cases), precision=HIGH)
    owned_count, coarse_total_rows = inverse_rows.shape
    indicator = (primal_map[:, None] == jnp.arange(coarse_total_rows)).astype(jnp.float32)
    owned_rhs = lax.psum_scatter(
        jnp.dot(indicator.T, coarse_local, precision=HIGH), "col", scatter_dimension=0, tiled=True
    )
    owned_rhs = lax.psum(owned_rhs, "row")
    columns = inverse_rows
    owned_solution = jnp.dot(
        columns, lax.all_gather(owned_rhs, "col", axis=0, tiled=True), precision=HIGH
    )
    columns = indicator
    own_coarse = jnp.dot(
        columns, lax.all_gather(owned_solution, "col", axis=0, tiled=True), precision=HIGH
    )
    coarse_back = jnp.dot(basis.T, own_coarse, precision=HIGH).reshape(residual.shape)
    return assemble(((local_term + coarse_back) * weight)[None], faces)[0]


def per_device(
    solution,
    residual,
    prev_direction,
    prev_dot,
    face_lists,
    multiplicity,
    block_pattern,
    schur,
    neumann_inverse,
    coarse_basis,
    primal_map,
    coarse_inverse,
):
    faces = face_lists[0, 0]
    pattern = block_pattern[0, 0]
    weight = (1.0 / multiplicity[0, 0].astype(jnp.float32))[:, None, None]
    current = residual[0, 0]
    previous = prev_direction[0, 0]
    precond = precondition(
        current,
        weight,
        faces,
        pattern,
        neumann_inverse[0, 0],
        coarse_basis[0, 0],
        primal_map[0, 0],
        coarse_inverse,
    )
    local_precond_dot = jnp.sum(current * precond * weight, axis=(0, 1))
    precond_dot = lax.psum(local_precond_dot, ("row", "col"))
    direction_mix = precond_dot / prev_dot
    direction = precond + direction_mix * previous
    image = assemble(block_product(schur[0, 0], pattern, direction[None]), faces)[0]
    curvature = lax.psum(jnp.sum(direction * image * weight, axis=(0, 1)), ("row", "col"))
    step_size = precond_dot / curvature
    new_solution = solution[0, 0] + step_size * direction
    new_residual = current - step_size * image
    return (new_solution[None, None], new_residual[None, None], direction[None, None])


def solution(mesh):
    placed = (
        P("row", "col", None, None, None),
        P("row", "col", None, None, None),
        P("row", "col", None, None, None),
        P(),
        P("row", "col", None, None),
        P("row", "col", None),
        P("row", "col", None, None),
        P("row", "col", None, None, None, None),
        P("row", "col", None, None, None, None),
        P("row", "col", None, None),
        P("row", "col", None),
        P("col", None),
    )
    return jax.shard_map(
        per_device,
        mesh=mesh,
        in_specs=placed,
        out_specs=(
            P("row", "col", None, None, None),
            P("row", "col", None, None, None),
            P("row", "col", None, None, None),
        ),
        check_vma=False,
    )
```

profile of v0, /device:TPU:1, one launch (start us, length us, event | category | flops | bytes accessed | tf_op | source)
XLA Modules:
  0.0 597.9 jit_solution(11276702184320067996)
XLA Ops:
  7.2 0.0 copy-start
  7.2 0.0 reduce-scatter.2.cloned.1.call-start
  7.2 0.8 divide_bitcast_fusion
  8.0 1.5 broadcast_multiply_fusion
  9.5 1.5 fusion.35
  11.0 1.5 fusion.38
  12.5 0.0 reduce-scatter.2.cloned.1.call-update
  12.5 2.3 fusion.31
  14.9 0.1 copy.39
  14.9 0.1 reshape_squeeze.4
  15.1 3.6 gather_fusion
  18.7 2.2 bitcast_select_fusion.1
  20.9 0.0 copy-start.9
  20.9 6.2 %fusion.6 = f32[1,16,128,128]{2,3,1,0:T(8,128)} fusion(f32[16,3,128,128]{3,2,1,0:T(8,128)S(1)} %bitcast.147, f32[1,1,16,3,128,128]{5,4,3,2,1,0:T(8,128)S(1)} %copy-done), kind=kOutput, calls=%fused_computation.15 | convolution fusion | flops 1207959552 | bytes 7340032 | tf_op jit(solution)/shard_map/bkij,vbkjn->vbin/dot_general | solution.py:30
  27.1 2.6 copy.44
  29.7 194.6 %reduce-scatter.2.cloned.1.call-done = f32[32,128]{1,0:T(8,128)} async-done(((f32[1024,128]{1,0:T(8,128)}), f32[32,128]{1,0:T(8,128)}) %reduce-scatter.2.cloned.1.call-update) | async-done | bytes 16400 | tf_op jit(solution)/shard_map/reduce_scatter | solution.py:52
  224.3 26.4 %psum.21 = f32[32,128]{1,0:T(8,128)S(1)} all-reduce(f32[32,128]{1,0:T(8,128)} %reduce-scatter.2.cloned.1.call-done), channel_id=1, replica_groups=mesh['row'=8,'col'=32] {'row'}, use_global_device_ids=true, to_apply=%region_1.3 | all-reduce | flops 4096 | bytes 32768 | tf_op jit(solution)/shard_map/psum | solution.py:55
  250.7 35.9 %all_gather.6 = f32[1024,128]{1,0:T(8,128)S(1)} all-gather(f32[32,128]{1,0:T(8,128)S(1)} %psum.21), channel_id=1, replica_groups=mesh['row'=8,'col'=32] {'col'}, dimensions={0}, use_global_device_ids=true | all-gather | bytes 540672 | tf_op jit(solution)/shard_map/all_gather | solution.py:58
  286.5 0.4 convolution_bitcast_fusion.5
  286.9 0.0 copy-start.10
  287.0 35.8 %all_gather.7 = f32[1024,128]{1,0:T(8,128)S(1)} all-gather(f32[32,128]{1,0:T(8,128)S(1)} %convolution_bitcast_fusion.5), channel_id=1, replica_groups=mesh['row'=8,'col'=32] {'col'}, dimensions={0}, use_global_device_ids=true | all-gather | bytes 540672 | tf_op jit(solution)/shard_map/all_gather | solution.py:62
  322.7 0.3 fusion.37
  323.0 2.0 convolution_bitcast_fusion.4
  325.0 2.5 copy.42
  327.6 2.4 reshape.184
  329.9 3.0 convolution_bitcast_fusion.3
  333.0 0.9 fusion.48
  333.9 27.6 %collective-permute-start = (f32[1,1,4,16384]{3,2,0,1:T(4,128)}, f32[1,1,4,16384]{3,2,0,1:T(4,128)}, u32[]{:S(2)}, u32[]{:S(2)}) collective-permute-start(f32[1,1,4,16384]{3,2,0,1:T(4,128)} %get-tuple-element.10), channel_id=1, source_target_pairs={{0,32},{32,64},{64,96},{96,128},{128,160},{160,192},{192,224},{1,3... | collective-permute-start | bytes 786440 | tf_op jit(solution)/shard_map/ppermute | solution.py:17
  361.5 3.8 collective-permute-start.1
  365.4 3.1 collective-permute-start.2
  368.4 1.3 collective-permute-start.3
  369.7 2.5 copy.41
  372.2 2.4 squeeze.32
  374.6 2.4 reshape.183
  377.0 1.6 collective-permute-done.3
  378.6 3.4 fusion.1
  382.0 0.0 copy-start.4
  382.0 0.0 copy-start.13
  382.0 0.9 copy-done.4
  383.0 0.2 copy.54
  383.2 1.0 copy-done.2
  384.1 0.4 fusion.14
  384.5 78.4 %psum.22 = f32[128]{0:T(128)S(1)} all-reduce(f32[128]{0:T(128)S(1)} %fusion.14), channel_id=1, replica_groups=mesh['row'=8,'col'=32] {'row','col'}, use_global_device_ids=true, to_apply=%region_3.5 | all-reduce | flops 128 | bytes 1024 | tf_op jit(solution)/shard_map/psum | solution.py:98
  462.9 2.7 fusion.12
  465.5 3.6 gather_fusion.1
  469.1 2.3 bitcast_select_fusion
  471.5 0.5 copy-done.7
  472.0 6.3 %fusion.9 = f32[1,16,128,128]{2,3,1,0:T(8,128)} fusion(f32[16,3,128,128]{3,2,1,0:T(8,128)S(1)} %bitcast.146, f32[1,1,16,3,128,128]{5,4,3,2,1,0:T(8,128)S(1)} %copy-done.7), kind=kOutput, calls=%fused_computation.16 | convolution fusion | flops 1207959552 | bytes 7340032 | tf_op jit(solution)/shard_map/bkij,vbkjn->vbin/dot_general | solution.py:30
  478.3 2.5 copy.47
  480.8 2.4 reshape.224
  483.2 2.4 reshape.187
  485.6 2.4 convolution_bitcast_fusion.1
  488.0 0.1 fusion.47
  488.1 3.7 collective-permute-start.4
  491.8 1.9 collective-permute-start.5
  493.7 1.9 collective-permute-start.6
  495.7 1.3 collective-permute-start.7
  497.0 2.5 collective-permute-done.5
  499.5 2.2 collective-permute-done.6
  501.7 4.1 collective-permute-done.7
  505.8 1.2 multiply_reduce_fusion
  507.0 1.2 copy.57
  508.2 78.4 %psum.23 = f32[128]{0:T(128)S(1)} all-reduce(f32[128]{0:T(128)S(1)} %bitcast_reduce_fusion), channel_id=1, replica_groups=mesh['row'=8,'col'=32] {'row','col'}, use_global_device_ids=true, to_apply=%region_6.8 | all-reduce | flops 128 | bytes 1024 | tf_op jit(solution)/shard_map/psum | solution.py:102
  586.6 4.5 multiply_add_fusion
  (31 shorter events, 0.1 us)
Async XLA Ops:
  7.2 13.7 %copy-start = (f32[1,1,16,3,128,128]{5,4,3,2,1,0:T(8,128)S(1)}, f32[1,1,16,3,128,128]{5,4,3,2,1,0:T(8,128)}, u32[]{:S(2)}) copy-start(f32[1,1,16,3,128,128]{5,4,3,2,1,0:T(8,128)} %param.22) | copy-start | bytes 9437188
  7.2 3.8 copy-start.11
  7.2 217.1 %reduce-scatter.2.cloned.1.call-start = ((), (), s32[]{:S(2)}) async-start(), calls=%async_computation.1 | async-start | bytes 540672 | tf_op jit(solution)/shard_map/reduce_scatter | solution.py:52
  8.0 6.8 %copy-start.12 = (s32[1,1,16,3]{2,1,3,0:T(1,128)S(1)}, s32[1,1,16,3]{2,1,3,0:T(1,128)}, u32[]{:S(2)}) copy-start(s32[1,1,16,3]{2,1,3,0:T(1,128)} %param.20) | copy-start | bytes 580
  20.9 265.7 %copy-start.9 = (f32[32,1024]{1,0:T(8,128)S(1)}, f32[32,1024]{1,0:T(8,128)}, u32[]{:S(2)}) copy-start(f32[32,1024]{1,0:T(8,128)} %param.25) | copy-start | bytes 393220
  27.1 295.9 %copy-start.8 = (f32[1,1,8,2048]{3,2,1,0:T(8,128)S(1)}, f32[1,1,8,2048]{3,2,1,0:T(8,128)}, u32[]{:S(2)}) copy-start(f32[1,1,8,2048]{3,2,1,0:T(8,128)} %param.23) | copy-start | bytes 196612
  286.9 43.0 %copy-start.10 = (s32[1,1,4,4]{3,2,1,0:T(4,128)S(1)}, s32[1,1,4,4]{3,2,1,0:T(4,128)}, u32[]{:S(2)}) copy-start(s32[1,1,4,4]{3,2,1,0:T(4,128)} %param.18) | copy-start | bytes 196
  333.9 43.1 %collective-permute-start = (f32[1,1,4,16384]{3,2,0,1:T(4,128)}, f32[1,1,4,16384]{3,2,0,1:T(4,128)}, u32[]{:S(2)}, u32[]{:S(2)}) collective-permute-start(f32[1,1,4,16384]{3,2,0,1:T(4,128)} %get-tuple-element.10), channel_id=1, source_target_pairs={{0,32},{32,64},{64,96},{96,128},{128,160},{160,192},{192,224},{1,3... | collective-permute-start | bytes 786440 | tf_op jit(solution)/shard_map/ppermute | solution.py:17
  361.5 15.5 %collective-permute-start.1 = (f32[1,1,4,16384]{3,2,0,1:T(4,128)}, f32[1,1,4,16384]{3,2,0,1:T(4,128)}, u32[]{:S(2)}, u32[]{:S(2)}) collective-permute-start(f32[1,1,4,16384]{3,2,0,1:T(4,128)} %get-tuple-element.13), channel_id=1, source_target_pairs={{32,0},{64,32},{96,64},{128,96},{160,128},{192,160},{224,192},{33,... | collective-permute-start | bytes 786440 | tf_op jit(solution)/shard_map/ppermute | solution.py:19
  365.4 11.7 %collective-permute-start.2 = (f32[1,1,4,16384]{3,2,0,1:T(4,128)}, f32[1,1,4,16384]{3,2,0,1:T(4,128)}, u32[]{:S(2)}, u32[]{:S(2)}) collective-permute-start(f32[1,1,4,16384]{3,2,0,1:T(4,128)} %get-tuple-element.12), channel_id=1, source_target_pairs={{0,1},{1,2},{2,3},{3,4},{4,5},{5,6},{6,7},{7,8},{8,9},{9,10},{10,1... | collective-permute-start | bytes 786440 | tf_op jit(solution)/shard_map/ppermute | solution.py:17
  368.4 10.2 %collective-permute-start.3 = (f32[1,1,4,16384]{3,2,0,1:T(4,128)S(1)}, f32[1,1,4,16384]{3,2,0,1:T(4,128)}, u32[]{:S(2)}, u32[]{:S(2)}) collective-permute-start(f32[1,1,4,16384]{3,2,0,1:T(4,128)S(1)} %get-tuple-element.11), channel_id=1, source_target_pairs={{1,0},{2,1},{3,2},{4,3},{5,4},{6,5},{7,6},{8,7},{9,8},{10,9},{11,1... | collective-permute-start | bytes 786440 | tf_op jit(solution)/shard_map/ppermute | solution.py:19
  378.6 5.5 copy-start.1
  382.0 1.0 copy-start.4
  382.0 80.9 %copy-start.13 = (f32[128]{0:T(128)S(1)}, f32[128]{0:T(128)}, u32[]{:S(2)}) copy-start(f32[128]{0:T(128)} %param.17) | copy-start | bytes 1540
  383.2 1.0 copy-start.2
  469.1 2.8 copy-start.7
  485.6 20.1 %copy-start.3 = (f32[1,16,16384]{2,1,0:T(8,128)S(1)}, f32[1,16,16384]{2,1,0:T(8,128)}, u32[]{:S(2)}) copy-start(f32[1,16,16384]{2,1,0:T(8,128)} %squeeze.32) | copy-start | bytes 3145732
  485.6 20.1 %copy-start.5 = (f32[1,16,16384]{2,1,0:T(8,128)S(1)}, f32[1,16,16384]{2,1,0:T(8,128)}, u32[]{:S(2)}) copy-start(f32[1,16,16384]{2,1,0:T(8,128)} %copy-done.4) | copy-start | bytes 3145732
  485.6 20.1 %copy-start.6 = (f32[1,16,16384]{2,1,0:T(8,128)S(1)}, f32[1,16,16384]{2,1,0:T(8,128)}, u32[]{:S(2)}) copy-start(f32[1,16,16384]{2,1,0:T(8,128)} %reshape.187) | copy-start | bytes 3145732
  488.1 8.9 %collective-permute-start.4 = (f32[1,1,4,16384]{3,2,0,1:T(4,128)S(1)}, f32[1,1,4,16384]{3,2,0,1:T(4,128)S(1)}, u32[]{:S(2)}, u32[]{:S(2)}) collective-permute-start(f32[1,1,4,16384]{3,2,0,1:T(4,128)S(1)} %get-tuple-element.6), channel_id=1, source_target_pairs={{0,32},{32,64},{64,96},{96,128},{128,160},{160,192},{192,224},{1,3... | collective-permute-start | bytes 786440 | tf_op jit(solution)/shard_map/ppermute | solution.py:17
  491.8 7.7 %collective-permute-start.5 = (f32[1,1,4,16384]{3,2,0,1:T(4,128)S(1)}, f32[1,1,4,16384]{3,2,0,1:T(4,128)S(1)}, u32[]{:S(2)}, u32[]{:S(2)}) collective-permute-start(f32[1,1,4,16384]{3,2,0,1:T(4,128)S(1)} %get-tuple-element.9), channel_id=1, source_target_pairs={{32,0},{64,32},{96,64},{128,96},{160,128},{192,160},{224,192},{33,... | collective-permute-start | bytes 786440 | tf_op jit(solution)/shard_map/ppermute | solution.py:19
  493.7 7.9 %collective-permute-start.6 = (f32[1,1,4,16384]{3,2,0,1:T(4,128)S(1)}, f32[1,1,4,16384]{3,2,0,1:T(4,128)S(1)}, u32[]{:S(2)}, u32[]{:S(2)}) collective-permute-start(f32[1,1,4,16384]{3,2,0,1:T(4,128)S(1)} %get-tuple-element.8), channel_id=1, source_target_pairs={{0,1},{1,2},{2,3},{3,4},{4,5},{5,6},{6,7},{7,8},{8,9},{9,10},{10,1... | collective-permute-start | bytes 786440 | tf_op jit(solution)/shard_map/ppermute | solution.py:17
  495.7 10.1 %collective-permute-start.7 = (f32[1,1,4,16384]{3,2,0,1:T(4,128)S(1)}, f32[1,1,4,16384]{3,2,0,1:T(4,128)S(1)}, u32[]{:S(2)}, u32[]{:S(2)}) collective-permute-start(f32[1,1,4,16384]{3,2,0,1:T(4,128)S(1)} %get-tuple-element.7), channel_id=1, source_target_pairs={{1,0},{2,1},{3,2},{4,3},{5,4},{6,5},{7,6},{8,7},{9,8},{10,9},{11,1... | collective-permute-start | bytes 786440 | tf_op jit(solution)/shard_map/ppermute | solution.py:19
Sparse Core Ops, SparseCore 0:
  12.7 211.5 reduce-scatter.1
where the time goes:
time: 599 us; the launch traced here: 598 us
  blocking collectives  255 us (43%)
  waiting for transfers between devices  205 us (34%)
  starting transfers between devices  44.6 us (7%)
  local copies, waits for them, and re-layouts  34.4 us (6%)
  matrix products  28.1 us (5%)
  other arithmetic  16.6 us (3%)
  between operations  14.3 us (2%)
    reduce_scatter x1, waiting for transfers between devices, precondition(): lax.psum_scatter(jnp.dot(indicator.T, coarse_local, precision=HIGH), 'col...  195 us
    psum x1, blocking collectives, per_device(): lax.psum(jnp.sum(direction * image * weight, axis=(0, 1)), ('row', 'col'))  78.4 us
    psum x1, blocking collectives, per_device(): precond_dot = lax.psum(local_precond_dot, ('row', 'col'))  78.4 us
    ppermute x4, starting transfers between devices, extended(): lax.ppermute(tail, axis, [(i, (i + 1) % count) for i in range(ends)])  36.3 us
    all_gather x1, blocking collectives, precondition(): lax.all_gather(owned_rhs, 'col', axis=0, tiled=True)  35.9 us
    all_gather x1, blocking collectives, precondition(): lax.all_gather(owned_solution, 'col', axis=0, tiled=True)  35.8 us
    psum x1, blocking collectives, precondition(): owned_rhs = lax.psum(owned_rhs, 'row')  26.4 us
    dot_general x2, matrix products, block_product(): return jnp.einsum('bkij,vbkjn->vbin', blocks, gathered, precision=HIGH)  12.5 us
  transfers between devices with their start and end apart: 9, of which 5 were waited for; matrix products, arithmetic and copies ran while one was open for 4% of the time, Pallas kernels for 0%

commit v1 on v0

--- a/solution.py
+++ b/solution.py
@@ -95,7 +95,7 @@
         coarse_inverse,
     )
     local_precond_dot = jnp.sum(current * precond * weight, axis=(0, 1))
-    precond_dot = lax.psum(local_precond_dot, ("row", "col"))
+    precond_dot = jnp.sum(lax.all_gather(local_precond_dot, ("row", "col")), axis=0)
     direction_mix = precond_dot / prev_dot
     direction = precond + direction_mix * previous
     image = assemble(block_product(schur[0, 0], pattern, direction[None]), faces)[0]

time: 599 us -> 577 us (0.963)
  blocking collectives: 255 us -> 232 us
    psum x1 -> x0, blocking collectives: 78.4 us -> none  [per_device(): precond_dot = lax.psum(local_precond_dot, ('row', 'col'))]
    all_gather x0 -> x1, blocking collectives: none -> 56.4 us  [per_device(): lax.all_gather(local_precond_dot, ('row', 'col'))]
where the time goes in v1:
time: 577 us; the launch traced here: 576 us
  blocking collectives  232 us (40%)
  waiting for transfers between devices  206 us (36%)
  starting transfers between devices  45.7 us (8%)
  local copies, waits for them, and re-layouts  33.2 us (6%)
  matrix products  28.1 us (5%)
  other arithmetic  16.9 us (3%)
  between operations  14.3 us (2%)
    reduce_scatter x1, waiting for transfers between devices, precondition(): lax.psum_scatter(jnp.dot(indicator.T, coarse_local, precision=HIGH), 'col...  195 us
    psum x1, blocking collectives, per_device(): lax.psum(jnp.sum(direction * image * weight, axis=(0, 1)), ('row', 'col'))  77.5 us
    all_gather x1, blocking collectives, per_device(): lax.all_gather(local_precond_dot, ('row', 'col'))  56.4 us
    ppermute x4, starting transfers between devices, extended(): lax.ppermute(tail, axis, [(i, (i + 1) % count) for i in range(ends)])  37.2 us
    all_gather x1, blocking collectives, precondition(): lax.all_gather(owned_rhs, 'col', axis=0, tiled=True)  35.9 us
    all_gather x1, blocking collectives, precondition(): lax.all_gather(owned_solution, 'col', axis=0, tiled=True)  35.8 us
    psum x1, blocking collectives, precondition(): owned_rhs = lax.psum(owned_rhs, 'row')  26.4 us
    dot_general x2, matrix products, block_product(): return jnp.einsum('bkij,vbkjn->vbin', blocks, gathered, precision=HIGH)  12.5 us
  transfers between devices with their start and end apart: 9, of which 5 were waited for; matrix products, arithmetic and copies ran while one was open for 4% of the time, Pallas kernels for 0%

profile of v1, /device:TPU:1, one launch (start us, length us, event | category | flops | bytes accessed | tf_op | source)
XLA Modules:
  0.0 576.0 jit_solution(15737009238192076865)
XLA Ops:
  7.2 0.0 copy-start
  7.2 0.0 reduce-scatter.2.cloned.1.call-start
  7.2 0.8 divide_bitcast_fusion
  8.0 1.5 broadcast_multiply_fusion
  9.5 1.5 fusion.35
  11.0 1.5 fusion.38
  12.5 0.0 reduce-scatter.2.cloned.1.call-update
  12.5 2.3 fusion.31
  14.9 0.1 copy.39
  14.9 0.1 reshape_squeeze.4
  15.1 3.6 gather_fusion
  18.7 2.2 bitcast_select_fusion.1
  20.9 0.0 copy-start.9
  20.9 6.2 %fusion.6 = f32[1,16,128,128]{2,3,1,0:T(8,128)} fusion(f32[16,3,128,128]{3,2,1,0:T(8,128)S(1)} %bitcast.148, f32[1,1,16,3,128,128]{5,4,3,2,1,0:T(8,128)S(1)} %copy-done), kind=kOutput, calls=%fused_computation.15 | convolution fusion | flops 1207959552 | bytes 7340032 | tf_op jit(solution)/shard_map/bkij,vbkjn->vbin/dot_general | solution.py:30
  27.1 2.6 copy.44
  29.7 194.6 %reduce-scatter.2.cloned.1.call-done = f32[32,128]{1,0:T(8,128)} async-done(((f32[1024,128]{1,0:T(8,128)}), f32[32,128]{1,0:T(8,128)}) %reduce-scatter.2.cloned.1.call-update) | async-done | bytes 16400 | tf_op jit(solution)/shard_map/reduce_scatter | solution.py:52
  224.3 26.4 %psum.14 = f32[32,128]{1,0:T(8,128)S(1)} all-reduce(f32[32,128]{1,0:T(8,128)} %reduce-scatter.2.cloned.1.call-done), channel_id=1, replica_groups=mesh['row'=8,'col'=32] {'row'}, use_global_device_ids=true, to_apply=%region_1.3 | all-reduce | flops 4096 | bytes 32768 | tf_op jit(solution)/shard_map/psum | solution.py:55
  250.7 35.9 %all_gather.12 = f32[1024,128]{1,0:T(8,128)S(1)} all-gather(f32[32,128]{1,0:T(8,128)S(1)} %psum.14), channel_id=1, replica_groups=mesh['row'=8,'col'=32] {'col'}, dimensions={0}, use_global_device_ids=true | all-gather | bytes 540672 | tf_op jit(solution)/shard_map/all_gather | solution.py:58
  286.5 0.4 convolution_bitcast_fusion.5
  286.9 0.0 copy-start.10
  287.0 35.8 %all_gather.13 = f32[1024,128]{1,0:T(8,128)S(1)} all-gather(f32[32,128]{1,0:T(8,128)S(1)} %convolution_bitcast_fusion.5), channel_id=1, replica_groups=mesh['row'=8,'col'=32] {'col'}, dimensions={0}, use_global_device_ids=true | all-gather | bytes 540672 | tf_op jit(solution)/shard_map/all_gather | solution.py:62
  322.7 0.3 fusion.37
  323.0 2.0 convolution_bitcast_fusion.4
  325.0 2.5 copy.42
  327.6 2.4 reshape.184
  329.9 3.0 convolution_bitcast_fusion.3
  333.0 0.9 fusion.48
  333.9 27.6 %collective-permute-start = (f32[1,1,4,16384]{3,2,0,1:T(4,128)}, f32[1,1,4,16384]{3,2,0,1:T(4,128)}, u32[]{:S(2)}, u32[]{:S(2)}) collective-permute-start(f32[1,1,4,16384]{3,2,0,1:T(4,128)} %get-tuple-element.10), channel_id=1, source_target_pairs={{0,32},{32,64},{64,96},{96,128},{128,160},{160,192},{192,224},{1,3... | collective-permute-start | bytes 786440 | tf_op jit(solution)/shard_map/ppermute | solution.py:17
  361.5 3.8 collective-permute-start.1
  365.4 3.1 collective-permute-start.2
  368.4 1.3 collective-permute-start.3
  369.7 2.5 copy.41
  372.2 2.4 squeeze.32
  374.6 2.4 reshape.183
  377.0 1.6 collective-permute-done.3
  378.6 3.4 fusion.1
  382.0 0.0 copy-start.4
  382.0 0.0 copy-start.13
  382.0 0.2 copy.54
  382.2 0.4 fusion.14
  382.6 0.7 copy-done.2
  383.3 56.4 %all-gather.1 = f32[256,1,128]{2,1,0:T(1,128)S(1)} all-gather(f32[1,1,128]{2,1,0:T(1,128)S(1)} %bitcast.161), channel_id=2, replica_groups=mesh['row'=8,'col'=32] {'row','col'}, dimensions={0}, use_global_device_ids=true | all-gather | bytes 131584 | tf_op jit(solution)/shard_map/all_gather | solution.py:98
  439.7 0.3 reduce_sum.35
  440.0 2.7 fusion.12
  442.6 3.6 gather_fusion.1
  446.2 2.3 bitcast_select_fusion
  448.6 0.5 copy-done.7
  449.1 6.3 %fusion.9 = f32[1,16,128,128]{2,3,1,0:T(8,128)} fusion(f32[16,3,128,128]{3,2,1,0:T(8,128)S(1)} %bitcast.147, f32[1,1,16,3,128,128]{5,4,3,2,1,0:T(8,128)S(1)} %copy-done.7), kind=kOutput, calls=%fused_computation.16 | convolution fusion | flops 1207959552 | bytes 7340032 | tf_op jit(solution)/shard_map/bkij,vbkjn->vbin/dot_general | solution.py:30
  455.4 2.5 copy.47
  457.9 2.4 reshape.228
  460.3 2.4 reshape.187
  462.7 2.4 convolution_bitcast_fusion.1
  465.1 0.1 fusion.47
  465.2 5.2 collective-permute-start.4
  470.4 2.1 collective-permute-start.5
  472.5 1.3 collective-permute-start.6
  473.8 1.3 collective-permute-start.7
  475.2 3.0 collective-permute-done.5
  478.1 1.4 collective-permute-done.6
  479.5 5.2 collective-permute-done.7
  484.7 1.2 multiply_reduce_fusion
  485.9 1.2 copy.57
  487.1 77.5 %psum.15 = f32[128]{0:T(128)S(1)} all-reduce(f32[128]{0:T(128)S(1)} %bitcast_reduce_fusion), channel_id=1, replica_groups=mesh['row'=8,'col'=32] {'row','col'}, use_global_device_ids=true, to_apply=%region_6.8 | all-reduce | flops 128 | bytes 1024 | tf_op jit(solution)/shard_map/psum | solution.py:102
  564.7 4.5 multiply_add_fusion
  (32 shorter events, 0.1 us)
Async XLA Ops:
  7.2 13.7 %copy-start = (f32[1,1,16,3,128,128]{5,4,3,2,1,0:T(8,128)S(1)}, f32[1,1,16,3,128,128]{5,4,3,2,1,0:T(8,128)}, u32[]{:S(2)}) copy-start(f32[1,1,16,3,128,128]{5,4,3,2,1,0:T(8,128)} %param.22) | copy-start | bytes 9437188
  7.2 3.8 copy-start.11
  7.2 217.1 %reduce-scatter.2.cloned.1.call-start = ((), (), s32[]{:S(2)}) async-start(), calls=%async_computation.1 | async-start | bytes 540672 | tf_op jit(solution)/shard_map/reduce_scatter | solution.py:52
  8.0 6.8 %copy-start.12 = (s32[1,1,16,3]{2,1,3,0:T(1,128)S(1)}, s32[1,1,16,3]{2,1,3,0:T(1,128)}, u32[]{:S(2)}) copy-start(s32[1,1,16,3]{2,1,3,0:T(1,128)} %param.20) | copy-start | bytes 580
  20.9 265.7 %copy-start.9 = (f32[32,1024]{1,0:T(8,128)S(1)}, f32[32,1024]{1,0:T(8,128)}, u32[]{:S(2)}) copy-start(f32[32,1024]{1,0:T(8,128)} %param.25) | copy-start | bytes 393220
  27.1 295.9 %copy-start.8 = (f32[1,1,8,2048]{3,2,1,0:T(8,128)S(1)}, f32[1,1,8,2048]{3,2,1,0:T(8,128)}, u32[]{:S(2)}) copy-start(f32[1,1,8,2048]{3,2,1,0:T(8,128)} %param.23) | copy-start | bytes 196612
  286.9 43.0 %copy-start.10 = (s32[1,1,4,4]{3,2,1,0:T(4,128)S(1)}, s32[1,1,4,4]{3,2,1,0:T(4,128)}, u32[]{:S(2)}) copy-start(s32[1,1,4,4]{3,2,1,0:T(4,128)} %param.18) | copy-start | bytes 196
  333.9 43.1 %collective-permute-start = (f32[1,1,4,16384]{3,2,0,1:T(4,128)}, f32[1,1,4,16384]{3,2,0,1:T(4,128)}, u32[]{:S(2)}, u32[]{:S(2)}) collective-permute-start(f32[1,1,4,16384]{3,2,0,1:T(4,128)} %get-tuple-element.10), channel_id=1, source_target_pairs={{0,32},{32,64},{64,96},{96,128},{128,160},{160,192},{192,224},{1,3... | collective-permute-start | bytes 786440 | tf_op jit(solution)/shard_map/ppermute | solution.py:17
  361.5 15.5 %collective-permute-start.1 = (f32[1,1,4,16384]{3,2,0,1:T(4,128)}, f32[1,1,4,16384]{3,2,0,1:T(4,128)}, u32[]{:S(2)}, u32[]{:S(2)}) collective-permute-start(f32[1,1,4,16384]{3,2,0,1:T(4,128)} %get-tuple-element.13), channel_id=1, source_target_pairs={{32,0},{64,32},{96,64},{128,96},{160,128},{192,160},{224,192},{33,... | collective-permute-start | bytes 786440 | tf_op jit(solution)/shard_map/ppermute | solution.py:19
  365.4 11.7 %collective-permute-start.2 = (f32[1,1,4,16384]{3,2,0,1:T(4,128)}, f32[1,1,4,16384]{3,2,0,1:T(4,128)}, u32[]{:S(2)}, u32[]{:S(2)}) collective-permute-start(f32[1,1,4,16384]{3,2,0,1:T(4,128)} %get-tuple-element.12), channel_id=1, source_target_pairs={{0,1},{1,2},{2,3},{3,4},{4,5},{5,6},{6,7},{7,8},{8,9},{9,10},{10,1... | collective-permute-start | bytes 786440 | tf_op jit(solution)/shard_map/ppermute | solution.py:17
  368.4 10.2 %collective-permute-start.3 = (f32[1,1,4,16384]{3,2,0,1:T(4,128)S(1)}, f32[1,1,4,16384]{3,2,0,1:T(4,128)}, u32[]{:S(2)}, u32[]{:S(2)}) collective-permute-start(f32[1,1,4,16384]{3,2,0,1:T(4,128)S(1)} %get-tuple-element.11), channel_id=1, source_target_pairs={{1,0},{2,1},{3,2},{4,3},{5,4},{6,5},{7,6},{8,7},{9,8},{10,9},{11,1... | collective-permute-start | bytes 786440 | tf_op jit(solution)/shard_map/ppermute | solution.py:19
  378.6 3.6 copy-start.1
  382.0 1.3 copy-start.4
  382.0 58.0 %copy-start.13 = (f32[128]{0:T(128)S(1)}, f32[128]{0:T(128)}, u32[]{:S(2)}) copy-start(f32[128]{0:T(128)} %param.17) | copy-start | bytes 1540
  382.2 1.1 copy-start.2
  446.2 2.8 copy-start.7
  462.7 22.0 %copy-start.3 = (f32[1,16,16384]{2,1,0:T(8,128)S(1)}, f32[1,16,16384]{2,1,0:T(8,128)}, u32[]{:S(2)}) copy-start(f32[1,16,16384]{2,1,0:T(8,128)} %squeeze.32) | copy-start | bytes 3145732
  462.7 22.0 %copy-start.5 = (f32[1,16,16384]{2,1,0:T(8,128)S(1)}, f32[1,16,16384]{2,1,0:T(8,128)}, u32[]{:S(2)}) copy-start(f32[1,16,16384]{2,1,0:T(8,128)} %copy-done.4) | copy-start | bytes 3145732
  462.7 22.0 %copy-start.6 = (f32[1,16,16384]{2,1,0:T(8,128)S(1)}, f32[1,16,16384]{2,1,0:T(8,128)}, u32[]{:S(2)}) copy-start(f32[1,16,16384]{2,1,0:T(8,128)} %reshape.187) | copy-start | bytes 3145732
  465.2 9.9 %collective-permute-start.4 = (f32[1,1,4,16384]{3,2,0,1:T(4,128)S(1)}, f32[1,1,4,16384]{3,2,0,1:T(4,128)S(1)}, u32[]{:S(2)}, u32[]{:S(2)}) collective-permute-start(f32[1,1,4,16384]{3,2,0,1:T(4,128)S(1)} %get-tuple-element.6), channel_id=1, source_target_pairs={{0,32},{32,64},{64,96},{96,128},{128,160},{160,192},{192,224},{1,3... | collective-permute-start | bytes 786440 | tf_op jit(solution)/shard_map/ppermute | solution.py:17
  470.4 7.7 %collective-permute-start.5 = (f32[1,1,4,16384]{3,2,0,1:T(4,128)S(1)}, f32[1,1,4,16384]{3,2,0,1:T(4,128)S(1)}, u32[]{:S(2)}, u32[]{:S(2)}) collective-permute-start(f32[1,1,4,16384]{3,2,0,1:T(4,128)S(1)} %get-tuple-element.9), channel_id=1, source_target_pairs={{32,0},{64,32},{96,64},{128,96},{160,128},{192,160},{224,192},{33,... | collective-permute-start | bytes 786440 | tf_op jit(solution)/shard_map/ppermute | solution.py:19
  472.5 7.0 %collective-permute-start.6 = (f32[1,1,4,16384]{3,2,0,1:T(4,128)S(1)}, f32[1,1,4,16384]{3,2,0,1:T(4,128)S(1)}, u32[]{:S(2)}, u32[]{:S(2)}) collective-permute-start(f32[1,1,4,16384]{3,2,0,1:T(4,128)S(1)} %get-tuple-element.8), channel_id=1, source_target_pairs={{0,1},{1,2},{2,3},{3,4},{4,5},{5,6},{6,7},{7,8},{8,9},{9,10},{10,1... | collective-permute-start | bytes 786440 | tf_op jit(solution)/shard_map/ppermute | solution.py:17
  473.8 10.8 %collective-permute-start.7 = (f32[1,1,4,16384]{3,2,0,1:T(4,128)S(1)}, f32[1,1,4,16384]{3,2,0,1:T(4,128)S(1)}, u32[]{:S(2)}, u32[]{:S(2)}) collective-permute-start(f32[1,1,4,16384]{3,2,0,1:T(4,128)S(1)} %get-tuple-element.7), channel_id=1, source_target_pairs={{1,0},{2,1},{3,2},{4,3},{5,4},{6,5},{7,6},{8,7},{9,8},{10,9},{11,1... | collective-permute-start | bytes 786440 | tf_op jit(solution)/shard_map/ppermute | solution.py:19
Sparse Core Ops, SparseCore 0:
  12.7 211.5 reduce-scatter.1
